TPU v7x, 32 devices: a whole 2x2x4 slice. The times are simulated.
32 devices in a mesh: query: 4 (over y, x), cand: 2 (over core), tensor: 4 (over z).
Axes of the slice: x: 2, y: 2, z: 4, core: 2. Of those that a mesh axis runs over, the one named last changes fastest.
Arguments:
- cand_states: bfloat16 [8192, 2048], P(('query', 'cand'), 'tensor'), parts along dimension 0, may hold values from -6 to 6
- prefix_states: bfloat16 [256, 2048], P(('query', 'cand'), 'tensor'), parts along dimension 0, may hold values from -6 to 6
- norm_gain: float32 [2048], replicated, may hold values from 0.5 to 1.5
- w_query: bfloat16 [2048, 1024], P(None, 'tensor'), may hold values from -1 to 1
- w_key: bfloat16 [2048, 256], P(None, 'tensor'), may hold values from -1 to 1
- w_value: bfloat16 [2048, 256], P(None, 'tensor'), may hold values from -0.125 to 0.125
- w_out: bfloat16 [1024, 2048], P('tensor'), may hold values from -1.5 to 1.5
- cand_lengths: int32 [64], P(('query', 'cand')), parts along dimension 0, may hold values from 32 to 128, as said below
Outputs:
- attn_out: bfloat16 [8192, 2048], P(('query', 'cand', 'tensor')), parts along dimension 0
There are 4 independent parts, one for each index of `query`. A program takes and returns all parts, laid end to end along the dimension named above; an argument that names none is the same for every part. Nothing has to cross between parts.
Inputs may be any that keep to these rules, and one draw needn't show every extreme that they name: `cand_lengths`: some candidate has all 128 slots live.
All inputs are finite; a program needn't handle non-finite values.
Results may differ from a plain program's by a relative error of at most 0.013.
Values may be sent and summed in bfloat16 or wider, within the bound.
No kernel may reach another device: no remote copies, remote signals or barrier semaphores. Data moves between devices by JAX's collectives and lax.ppermute only.
A program may use at most 64 MiB of HBM per device.

v0:
```python
import jax
import jax.numpy as jnp
from jax import lax
from jax.sharding import PartitionSpec as P

epsilon = 1e-06
theta_base = 10000.0


def rotate(values, positions):
    half_size = values.shape[-1] // 2
    frequency = theta_base ** (-jnp.arange(half_size, dtype=jnp.float32) * 2.0 / values.shape[-1])
    angles = positions.astype(jnp.float32)[:, None] * frequency[None, :]
    cosine = jnp.cos(angles)
    sine_part = jnp.sin(angles)
    lower_half = values[:, :half_size]
    upper_half = values[:, half_size:]
    return jnp.concatenate(
        [
            lower_half * cosine - upper_half * sine_part,
            upper_half * cosine + lower_half * sine_part,
        ],
        axis=-1,
    )


def normalize(states, norm_gain):
    values = states.astype(jnp.float32)
    square = jnp.mean(values * values, axis=-1, keepdims=True)
    return (values * lax.rsqrt(square + epsilon) * norm_gain[None, :]).astype(jnp.bfloat16)


def self_scores_of(queries, cand_keys):
    scores = jnp.einsum("cqd,ckd->cqk", queries, cand_keys, preferred_element_type=jnp.float32)
    slots = jnp.arange(scores.shape[1], dtype=jnp.int32)
    causal = slots[:, None] >= slots[None, :]
    return jnp.where(causal[None], scores, -jnp.inf)


def body(cand_states, prefix_states, norm_gain, w_query, w_key, w_value, w_out, cand_lengths):
    cand_full, prefix_full = (
        lax.all_gather(cand_states, "tensor", axis=1, tiled=True),
        lax.all_gather(prefix_states, "tensor", axis=1, tiled=True),
    )
    normed_cand = normalize(cand_full, norm_gain)
    normed_prefix = normalize(prefix_full, norm_gain)
    cand_count = cand_lengths.shape[0]
    cand_len = cand_full.shape[0] // cand_count
    prefix_rows = prefix_full.shape[0]
    cand_groups = lax.axis_size("cand")
    tensor_size = lax.axis_size("tensor")
    prefix_len = prefix_rows * cand_groups
    head_size = w_query.shape[1]
    cand_pos = prefix_len + jnp.tile(jnp.arange(cand_len, dtype=jnp.int32), cand_count)
    cand_key = jnp.dot(normed_cand, w_key, preferred_element_type=jnp.float32).astype(jnp.bfloat16)
    cand_value = jnp.dot(normed_cand, w_value, preferred_element_type=jnp.float32).astype(
        jnp.bfloat16
    )
    prefix_key = jnp.dot(normed_prefix, w_key, preferred_element_type=jnp.float32).astype(
        jnp.bfloat16
    )
    prefix_value = jnp.dot(normed_prefix, w_value, preferred_element_type=jnp.float32).astype(
        jnp.bfloat16
    )
    query_rows = rotate(
        jnp.dot(normed_cand, w_query, preferred_element_type=jnp.float32), cand_pos
    ) * head_size ** (-0.5)
    queries = query_rows.astype(jnp.bfloat16).reshape(cand_count, cand_len, head_size)
    cand_key, cand_value = (
        lax.all_gather(cand_key, "tensor", axis=1, tiled=True),
        lax.all_gather(cand_value, "tensor", axis=1, tiled=True),
    )
    key_pieces, value_pieces = (
        lax.all_gather(prefix_key, ("cand", "tensor"), axis=0, tiled=True),
        lax.all_gather(prefix_value, ("cand", "tensor"), axis=0, tiled=True),
    )

    def arrange(pieces):
        blocks = pieces.reshape(cand_groups, tensor_size, prefix_rows, pieces.shape[1])
        return blocks.transpose(0, 2, 1, 3).reshape(prefix_len, pieces.shape[1] * tensor_size)

    prefix_pos = jnp.arange(prefix_len, dtype=jnp.int32)
    prefix_keys = rotate(arrange(key_pieces).astype(jnp.float32), prefix_pos).astype(jnp.bfloat16)
    prefix_values = arrange(value_pieces)
    cand_keys = (
        rotate(cand_key.astype(jnp.float32), cand_pos)
        .astype(jnp.bfloat16)
        .reshape(cand_count, cand_len, head_size)
    )
    cand_values = cand_value.reshape(cand_count, cand_len, head_size)
    self_scores = self_scores_of(queries, cand_keys)
    prefix_scores = jnp.einsum(
        "cqd,kd->cqk", queries, prefix_keys, preferred_element_type=jnp.float32
    )
    highest = jnp.maximum(self_scores.max(-1), prefix_scores.max(-1))
    self_weights = jnp.exp(self_scores - highest[..., None])
    prefix_weights = jnp.exp(prefix_scores - highest[..., None])
    divisor = self_weights.sum(-1) + prefix_weights.sum(-1)
    summed = jnp.einsum(
        "cqk,ckd->cqd",
        self_weights.astype(jnp.bfloat16),
        cand_values,
        preferred_element_type=jnp.float32,
    )
    summed = summed + jnp.einsum(
        "cqk,kd->cqd",
        prefix_weights.astype(jnp.bfloat16),
        prefix_values,
        preferred_element_type=jnp.float32,
    )
    slots = jnp.arange(cand_len, dtype=jnp.int32)
    live_rows = slots[None, :] < cand_lengths[:, None]
    head_rows = jnp.where(live_rows[..., None], summed / divisor[..., None], 0.0)
    head_rows = head_rows.reshape(cand_count * cand_len, head_size).astype(jnp.bfloat16)
    row_count = head_rows.shape[0] // tensor_size
    all_heads = lax.all_to_all(head_rows, "tensor", split_axis=0, concat_axis=1, tiled=True)
    full_out = lax.all_gather(w_out, "tensor", axis=0, tiled=True)
    summed_out = jnp.zeros((row_count, full_out.shape[1]), jnp.float32)
    for head_index in range(tensor_size):
        head_term = jnp.dot(
            all_heads[:, head_index * head_size : (head_index + 1) * head_size],
            full_out[head_index * head_size : (head_index + 1) * head_size],
            preferred_element_type=jnp.float32,
        )
        summed_out = summed_out + lax.optimization_barrier(head_term.astype(jnp.bfloat16)).astype(
            jnp.float32
        )
    return summed_out.astype(jnp.bfloat16)


def solution(mesh):
    in_specs = (
        P(("query", "cand"), "tensor"),
        P(("query", "cand"), "tensor"),
        P(),
        P(None, "tensor"),
        P(None, "tensor"),
        P(None, "tensor"),
        P("tensor", None),
        P(("query", "cand")),
    )
    out_specs = P(("query", "cand", "tensor"), None)
    return jax.shard_map(body, mesh=mesh, in_specs=in_specs, out_specs=out_specs, check_vma=False)
```

profile of v0, /device:TPU:0, one launch (start us, length us, event | category | flops | bytes accessed | tf_op | source)
XLA Modules:
  0.0 214.7 jit_solution(11699257511544938787)
XLA Ops:
  6.5 0.0 copy-start
  6.5 0.0 all-gather.3.cloned.1.call-start
  6.5 0.7 all-gather.3.cloned.1.call-update
  7.3 0.0 all-gather.5.cloned.1.call-start
  7.3 0.7 all-gather.5.cloned.1.call-update
  8.0 15.3 %all_gather.23 = bf16[32,2048]{1,0:T(8,128)(2,1)S(1)} all-gather(bf16[32,512]{1,0:T(8,128)(2,1)} %param.9), channel_id=1, replica_groups=mesh['query'=4,'cand'=2,'tensor'=4] {'tensor'}, dimensions={1}, use_global_device_ids=true | all-gather | bytes 163840 | tf_op jit(solution)/shard_map/all_gather | solution.py:43
  23.3 0.1 fusion.30
  23.5 1.2 convolution_convert_fusion.7
  24.7 26.7 %all_gather.24 = bf16[256,64]{1,0:T(8,128)(2,1)S(1)} all-gather(bf16[32,64]{1,0:T(8,128)(2,1)S(1)} %convolution_convert_fusion.7), channel_id=1, replica_groups=mesh['query'=4,'cand'=2,'tensor'=4] {'cand','tensor'}, dimensions={0}, use_global_device_ids=true | all-gather | bytes 36864 | tf_op jit(solution)/shard_map/all_gather | solution.py:74
  51.4 0.1 copy.21
  51.5 0.1 reshape.111
  51.6 1.2 convolution_convert_fusion.6
  52.8 27.9 %all_gather.26 = bf16[256,64]{1,0:T(8,128)(2,1)S(1)} all-gather(bf16[32,64]{1,0:T(8,128)(2,1)S(1)} %convolution_convert_fusion.6), channel_id=1, replica_groups=mesh['query'=4,'cand'=2,'tensor'=4] {'cand','tensor'}, dimensions={0}, use_global_device_ids=true | all-gather | bytes 36864 | tf_op jit(solution)/shard_map/all_gather | solution.py:75
  80.8 0.1 reshape.114
  81.0 0.0 copy-done.7
  81.0 0.1 iota_compare_fusion.1
  81.1 0.2 fusion.51
  81.3 13.3 %all-gather.3.cloned.1.call-done = bf16[1024,2048]{1,0:T(8,128)(2,1)} async-done(((bf16[1024,512]{1,0:T(8,128)(2,1)}), bf16[1024,2048]{1,0:T(8,128)(2,1)}) %all-gather.3.cloned.1.call-update) | async-done | bytes 4194320 | tf_op jit(solution)/shard_map/all_gather | solution.py:42
  94.6 3.2 %fusion = f32[1024]{0:T(1024)S(1)} fusion(bf16[1024,2048]{1,0:T(8,128)(2,1)} %all-gather.3.cloned.1.call-done), kind=kLoop, calls=%fused_computation.2 | loop fusion | flops 6290432 | bytes 4198400 | tf_op jit(solution)/shard_map/reduce_sum | solution.py:29
  97.8 0.0 copy-done.6
  97.8 0.2 copy-done.2
  98.0 1.0 fusion.2
  99.0 0.0 copy-start.1
  99.1 2.0 copy-done.1
  101.0 1.4 convolution_convert_fusion.5
  102.4 21.4 %all_gather.22 = bf16[1024,256]{0,1:T(8,128)(2,1)S(1)} all-gather(bf16[1024,64]{0,1:T(8,128)(2,1)S(1)} %convolution_convert_fusion.5), channel_id=1, replica_groups=mesh['query'=4,'cand'=2,'tensor'=4] {'tensor'}, dimensions={1}, use_global_device_ids=true | all-gather | bytes 655360 | tf_op jit(solution)/shard_map/all_gather | solution.py:70
  123.8 0.2 copy.20
  124.0 0.1 convert_element_type.144
  124.1 3.6 %convolution_convert_fusion.4 = bf16[1024,64]{0,1:T(8,128)(2,1)S(1)} fusion(bf16[1024,2048]{1,0:T(8,128)(2,1)} %copy-done.1, bf16[2048,64]{0,1:T(8,128)(2,1)S(1)} %copy-done.5), kind=kOutput, calls=%fused_computation.15 | convolution fusion | flops 268500992 | bytes 4587520 | tf_op jit(solution)/shard_map/dot_general | solution.py:56
  127.7 21.3 %all_gather.25 = bf16[1024,256]{0,1:T(8,128)(2,1)S(1)} all-gather(bf16[1024,64]{0,1:T(8,128)(2,1)S(1)} %convolution_convert_fusion.4), channel_id=1, replica_groups=mesh['query'=4,'cand'=2,'tensor'=4] {'tensor'}, dimensions={1}, use_global_device_ids=true | all-gather | bytes 655360 | tf_op jit(solution)/shard_map/all_gather | solution.py:71
  149.0 0.2 copy.27
  149.2 3.5 %fusion.67 = f32[1024,256]{1,0:T(8,128)S(1)} fusion(bf16[1024,2048]{1,0:T(8,128)(2,1)} %copy-done.1, bf16[2048,256]{1,0:T(8,128)(2,1)S(1)} %copy-done), kind=kOutput, calls=%fused_computation.92 | convolution fusion | flops 1073741824 | bytes 6291456 | tf_op jit(solution)/shard_map/dot_general | solution.py:66
  152.7 2.5 %fusion.19 = (f32[1024,128]{1,0:T(8,128)S(1)}, f32[1024,128]{1,0:T(8,128)S(1)}, bf16[1024,128]{1,0:T(8,128)(2,1)S(1)}, bf16[1024,128]{1,0:T(8,128)(2,1)S(1)}) fusion(f32[1024,256]{1,0:T(8,128)S(1)} %fusion.67, f32[128]{0:T(128)S(1)} %multiply_power_fusion, f32[1024]{0:T(1024)S(1)} %convert_bitcast_fusion.1, f32[1024,256]{1,0:T(8,128)S(1)} %convert_element_type.144), kind=kLoop, calls=%fused_computation.35 | loop fusion | flops 1966080 | bytes 3674624 | tf_op jit(solution)/shard_map/sub | solution.py:20
  155.2 0.3 fusion.66
  155.5 0.3 fusion.65
  155.8 0.1 fusion.36
  155.9 0.1 fusion.28
  156.0 0.3 fusion.33
  156.3 0.4 fusion.5
  156.8 1.0 copy.25
  157.8 5.3 %all-to-all-start = ((bf16[4,256,256]{1,2,0:T(8,128)(2,1)}), bf16[4,256,256]{1,2,0:T(8,128)(2,1)S(1)}, u32[]{:S(2)}, u32[]{:S(2)}) async-start(bf16[4,256,256]{1,2,0:T(8,128)(2,1)} %copy.25), calls=%async_computation | async-start | bytes 1048576 | tf_op jit(solution)/shard_map/all_to_all | solution.py:116
  163.1 38.6 %all-gather.5.cloned.1.call-done = bf16[1024,2048]{1,0:T(8,128)(2,1)} async-done(((bf16[256,2048]{1,0:T(8,128)(2,1)}), bf16[1024,2048]{1,0:T(8,128)(2,1)}) %all-gather.5.cloned.1.call-update) | async-done | bytes 4194320 | tf_op jit(solution)/shard_map/all_gather | solution.py:117
  201.7 0.0 all-to-all-done
  201.7 1.8 convolution_convert_fusion.3
  203.6 1.7 convolution_convert_fusion.2
  205.3 0.5 convolution_convert_fusion.1
  205.7 0.5 convolution_convert_fusion
  206.2 1.7 add_convert_fusion
  (20 shorter events, 0.1 us)
Async XLA Ops:
  6.5 142.7 %copy-start = (bf16[2048,256]{1,0:T(8,128)(2,1)S(1)}, bf16[2048,256]{1,0:T(8,128)(2,1)}, u32[]{:S(2)}) copy-start(bf16[2048,256]{1,0:T(8,128)(2,1)} %param.11) | copy-start | bytes 3145732
  6.5 91.3 %copy-start.6 = (f32[2048]{0:T(1024)S(1)}, f32[2048]{0:T(1024)}, u32[]{:S(2)}) copy-start(f32[2048]{0:T(1024)} %param.10) | copy-start | bytes 24580
  6.5 74.5 %copy-start.7 = (s32[8]{0:T(128)S(1)}, s32[8]{0:T(128)}, u32[]{:S(2)}) copy-start(s32[8]{0:T(128)} %param.15) | copy-start | bytes 100
  6.5 88.0 %all-gather.3.cloned.1.call-start = ((), (), s32[]{:S(2)}) async-start(), calls=%async_computation.1 | async-start | bytes 5242880 | tf_op jit(solution)/shard_map/all_gather | solution.py:42
  7.3 194.5 %all-gather.5.cloned.1.call-start = ((), (), s32[]{:S(2)}) async-start(), calls=%async_computation.2 | async-start | bytes 5242880 | tf_op jit(solution)/shard_map/all_gather | solution.py:117
  94.6 3.4 %copy-start.2 = (bf16[1024,2048]{1,0:T(8,128)(2,1)S(1)}, bf16[1024,2048]{1,0:T(8,128)(2,1)}, u32[]{:S(2)}) copy-start(bf16[1024,2048]{1,0:T(8,128)(2,1)} %all-gather.3.cloned.1.call-done) | copy-start | bytes 12582916
  98.0 3.0 %copy-start.4 = (bf16[2048,64]{0,1:T(8,128)(2,1)S(1)}, bf16[2048,64]{0,1:T(8,128)(2,1)}, u32[]{:S(2)}) copy-start(bf16[2048,64]{0,1:T(8,128)(2,1)} %param.12) | copy-start | bytes 786436
  99.0 2.0 copy-start.1
  101.0 23.0 %copy-start.5 = (bf16[2048,64]{0,1:T(8,128)(2,1)S(1)}, bf16[2048,64]{0,1:T(8,128)(2,1)}, u32[]{:S(2)}) copy-start(bf16[2048,64]{0,1:T(8,128)(2,1)} %param.13) | copy-start | bytes 786436
  157.8 44.0 %all-to-all-start = ((bf16[4,256,256]{1,2,0:T(8,128)(2,1)}), bf16[4,256,256]{1,2,0:T(8,128)(2,1)S(1)}, u32[]{:S(2)}, u32[]{:S(2)}) async-start(bf16[4,256,256]{1,2,0:T(8,128)(2,1)} %copy.25), calls=%async_computation | async-start | bytes 1048576 | tf_op jit(solution)/shard_map/all_to_all | solution.py:116
  201.7 3.5 %copy-start.3 = (bf16[1024,2048]{1,0:T(8,128)(2,1)S(1)}, bf16[1024,2048]{1,0:T(8,128)(2,1)}, u32[]{:S(2)}) copy-start(bf16[1024,2048]{1,0:T(8,128)(2,1)} %all-gather.5.cloned.1.call-done) | copy-start | bytes 12582916
Sparse Core Ops, SparseCore 0:
  8.9 85.6 all-gather.2
  96.1 105.5 all-gather.4
where the time goes:
time: 215 us
  blocking collectives  113 us (53%)
  waiting for transfers between devices  53.3 us (25%)
  matrix products  16.8 us (8%)
  between operations  13.6 us (6%)
  other arithmetic  9.09 us (4%)
  starting transfers between devices  5.36 us (2%)
  local copies, waits for them, and re-layouts  3.97 us (2%)
    all_gather x1, waiting for transfers between devices, body(): full_out = lax.all_gather(w_out, 'tensor', axis=0, tiled=True)  38.6 us
    all_gather x1, blocking collectives, body(): lax.all_gather(prefix_value, ('cand', 'tensor'), axis=0, tiled=True)  27.9 us
    all_gather x1, blocking collectives, body(): lax.all_gather(prefix_key, ('cand', 'tensor'), axis=0, tiled=True)  26.7 us
    all_gather x1, blocking collectives, body(): lax.all_gather(cand_key, 'tensor', axis=1, tiled=True)  21.4 us
    all_gather x1, blocking collectives, body(): lax.all_gather(cand_value, 'tensor', axis=1, tiled=True)  21.3 us
    all_gather x1, blocking collectives, body(): lax.all_gather(prefix_states, 'tensor', axis=1, tiled=True)  15.3 us
    all_gather x1, waiting for transfers between devices, body(): lax.all_gather(cand_states, 'tensor', axis=1, tiled=True)  13.3 us
    all_to_all x1, starting transfers between devices, body(): lax.all_to_all(head_rows, 'tensor', split_axis=0, concat_axis=1, tiled=True)  5.32 us
  transfers between devices with their start and end apart: 3, of which 2 were waited for; matrix products, arithmetic and copies ran while one was open for 10% of the time, Pallas kernels for 0%

commit v1 on v0

--- a/solution.py
+++ b/solution.py
@@ -38,6 +38,11 @@
 
 
 def body(cand_states, prefix_states, norm_gain, w_query, w_key, w_value, w_out, cand_lengths):
+
+    def _meet_corner(block_here, dim_i):
+        base_arr = lax.all_gather(block_here, "tensor")
+        return jnp.concatenate(base_arr, axis=dim_i)
+
     cand_full, prefix_full = (
         lax.all_gather(cand_states, "tensor", axis=1, tiled=True),
         lax.all_gather(prefix_states, "tensor", axis=1, tiled=True),
@@ -67,7 +72,7 @@
     ) * head_size ** (-0.5)
     queries = query_rows.astype(jnp.bfloat16).reshape(cand_count, cand_len, head_size)
     cand_key, cand_value = (
-        lax.all_gather(cand_key, "tensor", axis=1, tiled=True),
+        _meet_corner(cand_key, 1),
         lax.all_gather(cand_value, "tensor", axis=1, tiled=True),
     )
     key_pieces, value_pieces = (

time: 215 us -> 214 us (level)
  waiting for transfers between devices: 53.3 us -> 56.2 us
    all_gather x1, waiting for transfers between devices: 38.6 us -> 41.5 us  [body(): full_out = lax.all_gather(w_out, 'tensor', axis=0, tiled=True)]
where the time goes in v1:
time: 214 us
  blocking collectives  112 us (52%)
  waiting for transfers between devices  56.2 us (26%)
  matrix products  16.7 us (8%)
  between operations  13.7 us (6%)
  other arithmetic  9.1 us (4%)
  starting transfers between devices  3.68 us (2%)
  local copies, waits for them, and re-layouts  2.37 us (1%)
    all_gather x1, waiting for transfers between devices, body(): full_out = lax.all_gather(w_out, 'tensor', axis=0, tiled=True)  41.5 us
    all_gather x1, blocking collectives, body(): lax.all_gather(prefix_value, ('cand', 'tensor'), axis=0, tiled=True)  27.9 us
    all_gather x1, blocking collectives, body(): lax.all_gather(prefix_key, ('cand', 'tensor'), axis=0, tiled=True)  26.7 us
    all_gather x1, blocking collectives, body(): lax.all_gather(cand_value, 'tensor', axis=1, tiled=True)  22.5 us
    all_gather x1, blocking collectives, _meet_corner(): base_arr = lax.all_gather(block_here, 'tensor')  19.6 us
    all_gather x1, blocking collectives, body(): lax.all_gather(prefix_states, 'tensor', axis=1, tiled=True)  15.3 us
    all_gather x1, waiting for transfers between devices, body(): lax.all_gather(cand_states, 'tensor', axis=1, tiled=True)  13.3 us
    dot_general x4, matrix products, body(): jnp.dot(all_heads[:, head_index * head_size:(head_index + 1) * head_size]...  4.42 us
  transfers between devices with their start and end apart: 3, of which 2 were waited for; matrix products, arithmetic and copies ran while one was open for 10% of the time, Pallas kernels for 0%

profile of v1, /device:TPU:0, one launch (start us, length us, event | category | flops | bytes accessed | tf_op | source)
XLA Modules:
  0.0 213.7 jit_solution(2698247154895858642)
XLA Ops:
  6.5 0.7 all-gather.4.cloned.1.call-update
  7.3 0.0 all-gather.6.cloned.1.call-start
  7.3 0.7 all-gather.6.cloned.1.call-update
  8.0 15.3 %all_gather.27 = bf16[32,2048]{1,0:T(8,128)(2,1)S(1)} all-gather(bf16[32,512]{1,0:T(8,128)(2,1)} %param.9), channel_id=1, replica_groups=mesh['query'=4,'cand'=2,'tensor'=4] {'tensor'}, dimensions={1}, use_global_device_ids=true | all-gather | bytes 163840 | tf_op jit(solution)/shard_map/all_gather | solution.py:48
  23.3 0.1 fusion.30
  23.5 1.2 convolution_convert_fusion.7
  24.7 26.7 %all_gather.28 = bf16[256,64]{1,0:T(8,128)(2,1)S(1)} all-gather(bf16[32,64]{1,0:T(8,128)(2,1)S(1)} %convolution_convert_fusion.7), channel_id=1, replica_groups=mesh['query'=4,'cand'=2,'tensor'=4] {'cand','tensor'}, dimensions={0}, use_global_device_ids=true | all-gather | bytes 36864 | tf_op jit(solution)/shard_map/all_gather | solution.py:79
  51.4 1.2 convolution_convert_fusion.6
  52.6 0.1 copy.17
  52.7 0.1 reshape.116
  52.9 27.9 %all_gather.30 = bf16[256,64]{1,0:T(8,128)(2,1)S(1)} all-gather(bf16[32,64]{1,0:T(8,128)(2,1)S(1)} %convolution_convert_fusion.6), channel_id=1, replica_groups=mesh['query'=4,'cand'=2,'tensor'=4] {'cand','tensor'}, dimensions={0}, use_global_device_ids=true | all-gather | bytes 36864 | tf_op jit(solution)/shard_map/all_gather | solution.py:80
  80.8 0.1 reshape.121
  81.0 0.1 iota_compare_fusion.1
  81.1 0.2 fusion.51
  81.3 13.3 %all-gather.4.cloned.1.call-done = bf16[1024,2048]{1,0:T(8,128)(2,1)} async-done(((bf16[1024,512]{1,0:T(8,128)(2,1)}), bf16[1024,2048]{1,0:T(8,128)(2,1)}) %all-gather.4.cloned.1.call-update) | async-done | bytes 4194320 | tf_op jit(solution)/shard_map/all_gather | solution.py:47
  94.6 3.2 %fusion = f32[1024]{0:T(1024)S(1)} fusion(bf16[1024,2048]{1,0:T(8,128)(2,1)} %all-gather.4.cloned.1.call-done), kind=kLoop, calls=%fused_computation.2 | loop fusion | flops 6290432 | bytes 4198400 | tf_op jit(solution)/shard_map/reduce_sum | solution.py:29
  97.8 0.2 copy-done.2
  98.0 1.0 fusion.2
  99.0 0.0 copy-done.4
  99.1 0.0 copy-start.1
  99.1 1.4 convolution_convert_fusion.5
  100.5 0.0 copy-start.5
  100.5 19.6 %all-gather = bf16[4096,64]{0,1:T(8,128)(2,1)S(1)} all-gather(bf16[1024,64]{0,1:T(8,128)(2,1)S(1)} %convolution_convert_fusion.5), channel_id=2, replica_groups=mesh['query'=4,'cand'=2,'tensor'=4] {'tensor'}, dimensions={0}, use_global_device_ids=true | all-gather | bytes 655360 | tf_op jit(solution)/shard_map/all_gather | solution.py:43
  120.0 0.1 convert_element_type.181
  120.1 0.1 copy.28
  120.2 0.1 fusion.65
  120.3 0.2 copy.24
  120.5 0.2 copy.25
  120.7 3.6 %convolution_convert_fusion.4 = bf16[1024,64]{0,1:T(8,128)(2,1)S(1)} fusion(bf16[1024,2048]{1,0:T(8,128)(2,1)} %copy-done.1, bf16[2048,64]{0,1:T(8,128)(2,1)S(1)} %copy-done.5), kind=kOutput, calls=%fused_computation.15 | convolution fusion | flops 268500992 | bytes 4587520 | tf_op jit(solution)/shard_map/dot_general | solution.py:61
  124.3 22.5 %all_gather.29 = bf16[1024,256]{0,1:T(8,128)(2,1)S(1)} all-gather(bf16[1024,64]{0,1:T(8,128)(2,1)S(1)} %convolution_convert_fusion.4), channel_id=1, replica_groups=mesh['query'=4,'cand'=2,'tensor'=4] {'tensor'}, dimensions={1}, use_global_device_ids=true | all-gather | bytes 655360 | tf_op jit(solution)/shard_map/all_gather | solution.py:76
  146.8 0.2 copy.23
  147.0 3.5 %fusion.68 = f32[1024,256]{1,0:T(8,128)S(1)} fusion(bf16[1024,2048]{1,0:T(8,128)(2,1)} %copy-done.1, bf16[2048,256]{1,0:T(8,128)(2,1)S(1)} %copy-done), kind=kOutput, calls=%fused_computation.94 | convolution fusion | flops 1073741824 | bytes 6291456 | tf_op jit(solution)/shard_map/dot_general | solution.py:71
  150.5 2.5 %fusion.19 = (f32[1024,128]{1,0:T(8,128)S(1)}, f32[1024,128]{1,0:T(8,128)S(1)}, bf16[1024,128]{1,0:T(8,128)(2,1)S(1)}, bf16[1024,128]{1,0:T(8,128)(2,1)S(1)}) fusion(f32[1024,256]{1,0:T(8,128)S(1)} %fusion.68, f32[128]{0:T(128)S(1)} %multiply_power_fusion, f32[1024]{0:T(1024)S(1)} %convert_bitcast_fusion.1, f32[1024,128]{1,0:T(8,128)S(1)} %copy.24, ...), kind=kLoop, calls=%fused_computation.36 | loop fusion | flops 1966080 | bytes 3674624 | tf_op jit(solution)/shard_map/sub | solution.py:20
  153.0 0.3 fusion.67
  153.3 0.3 fusion.66
  153.6 0.1 fusion.36
  153.7 0.1 fusion.28
  153.8 0.4 fusion.33
  154.2 0.4 fusion.5
  154.6 1.0 copy.21
  155.6 3.6 %all-to-all-start = ((bf16[4,256,256]{1,2,0:T(8,128)(2,1)}), bf16[4,256,256]{1,2,0:T(8,128)(2,1)S(1)}, u32[]{:S(2)}, u32[]{:S(2)}) async-start(bf16[4,256,256]{1,2,0:T(8,128)(2,1)} %copy.21), calls=%async_computation | async-start | bytes 1048576 | tf_op jit(solution)/shard_map/all_to_all | solution.py:121
  159.2 41.5 %all-gather.6.cloned.1.call-done = bf16[1024,2048]{1,0:T(8,128)(2,1)} async-done(((bf16[256,2048]{1,0:T(8,128)(2,1)}), bf16[1024,2048]{1,0:T(8,128)(2,1)}) %all-gather.6.cloned.1.call-update) | async-done | bytes 4194320 | tf_op jit(solution)/shard_map/all_gather | solution.py:122
  200.7 0.0 all-to-all-done
  200.7 1.8 convolution_convert_fusion.3
  202.6 1.7 convolution_convert_fusion.2
  204.3 0.5 convolution_convert_fusion.1
  204.7 0.5 convolution_convert_fusion
  205.2 1.7 add_convert_fusion
  (23 shorter events, 0.1 us)
Async XLA Ops:
  6.5 140.5 %copy-start = (bf16[2048,256]{1,0:T(8,128)(2,1)S(1)}, bf16[2048,256]{1,0:T(8,128)(2,1)}, u32[]{:S(2)}) copy-start(bf16[2048,256]{1,0:T(8,128)(2,1)} %param.11) | copy-start | bytes 3145732
  6.5 91.3 %copy-start.6 = (f32[2048]{0:T(1024)S(1)}, f32[2048]{0:T(1024)}, u32[]{:S(2)}) copy-start(f32[2048]{0:T(1024)} %param.10) | copy-start | bytes 24580
  6.5 74.5 %copy-start.7 = (s32[8]{0:T(128)S(1)}, s32[8]{0:T(128)}, u32[]{:S(2)}) copy-start(s32[8]{0:T(128)} %param.15) | copy-start | bytes 100
  6.5 88.0 %all-gather.4.cloned.1.call-start = ((), (), s32[]{:S(2)}) async-start(), calls=%async_computation.1 | async-start | bytes 5242880 | tf_op jit(solution)/shard_map/all_gather | solution.py:47
  7.3 193.5 %all-gather.6.cloned.1.call-start = ((), (), s32[]{:S(2)}) async-start(), calls=%async_computation.2 | async-start | bytes 5242880 | tf_op jit(solution)/shard_map/all_gather | solution.py:122
  94.6 3.4 %copy-start.2 = (bf16[1024,2048]{1,0:T(8,128)(2,1)S(1)}, bf16[1024,2048]{1,0:T(8,128)(2,1)}, u32[]{:S(2)}) copy-start(bf16[1024,2048]{1,0:T(8,128)(2,1)} %all-gather.4.cloned.1.call-done) | copy-start | bytes 12582916
  98.0 1.0 copy-start.4
  99.1 21.2 %copy-start.1 = (bf16[1024,2048]{1,0:T(8,128)(2,1)}, bf16[1024,2048]{1,0:T(8,128)(2,1)S(1)}, u32[]{:S(2)}) copy-start(bf16[1024,2048]{1,0:T(8,128)(2,1)S(1)} %fusion.2) | copy-start | bytes 12582916
  100.5 20.2 %copy-start.5 = (bf16[2048,64]{0,1:T(8,128)(2,1)S(1)}, bf16[2048,64]{0,1:T(8,128)(2,1)}, u32[]{:S(2)}) copy-start(bf16[2048,64]{0,1:T(8,128)(2,1)} %param.13) | copy-start | bytes 786436
  155.6 45.1 %all-to-all-start = ((bf16[4,256,256]{1,2,0:T(8,128)(2,1)}), bf16[4,256,256]{1,2,0:T(8,128)(2,1)S(1)}, u32[]{:S(2)}, u32[]{:S(2)}) async-start(bf16[4,256,256]{1,2,0:T(8,128)(2,1)} %copy.21), calls=%async_computation | async-start | bytes 1048576 | tf_op jit(solution)/shard_map/all_to_all | solution.py:121
  200.7 3.5 %copy-start.3 = (bf16[1024,2048]{1,0:T(8,128)(2,1)S(1)}, bf16[1024,2048]{1,0:T(8,128)(2,1)}, u32[]{:S(2)}) copy-start(bf16[1024,2048]{1,0:T(8,128)(2,1)} %all-gather.6.cloned.1.call-done) | copy-start | bytes 12582916
Sparse Core Ops, SparseCore 0:
  8.9 85.6 all-gather.3
  96.1 104.5 all-gather.5
